TPU v7x, 32 devices: a whole 2x2x4 slice. The times are simulated.
32 devices in a mesh: top: 4 (over x, core), mid: 2 (over y), leaf: 4 (over z).
Axes of the slice: x: 2, y: 2, z: 4, core: 2. Of those that a mesh axis runs over, the one named last changes fastest.
Arguments:
- rhs: bfloat16 [49152, 256], P(('top', 'mid', 'leaf')), may hold values from -6 to 6
- guess: bfloat16 [49152, 256], P(('top', 'mid', 'leaf')), may hold values from -3 to 3
- diag_blocks: bfloat16 [32, 1536, 1536], P(('top', 'mid', 'leaf')), as said below
- precond: bfloat16 [32, 1536, 1536], P(('top', 'mid', 'leaf'))
- bases: bfloat16 [32, 1536, 128], P(('top', 'mid', 'leaf')), may hold values from -0.3125 to 0.3125
- leaf_to_middle_transfer: bfloat16 [32, 128, 128], P(('top', 'mid', 'leaf')), may hold values from -0.25 to 0.25
- mid_transfer: bfloat16 [8, 128, 128], replicated, may hold values from -0.375 to 0.375
- leaf_coupling: bfloat16 [32, 4, 128, 128], P(('top', 'mid', 'leaf')), may hold values from -0.25 to 0.25
- cluster_coupling: bfloat16 [8, 3, 128, 128], P(('top', 'mid')), may hold values from -0.3125 to 0.3125
- group_coupling: bfloat16 [4, 2, 128, 128], P('top'), may hold values from -0.375 to 0.375
- leaf_lists: int32 [32, 4], P(('top', 'mid', 'leaf')), may hold values from 0 to 3, as said below
- owner: int32 [8, 4], P(('top', 'mid')), may hold values from 0 to 3, as said below
- cluster_lists: int32 [8, 3], P(('top', 'mid')), may hold values from 0 to 7, as said below
- group_lists: int32 [4, 2], P('top'), may hold values from 0 to 3, as said below
Outputs:
- solution: bfloat16 [49152, 256], P(('top', 'mid', 'leaf'))
Inputs may be any that keep to these rules, and one draw needn't show every extreme that they name: `leaf_lists`: each row holds 4 distinct sibling cluster ids. `owner`: each row is a permutation of the slots of the cluster. `cluster_lists`: each row holds 3 distinct cluster ids. `group_lists`: each row holds 2 distinct group ids. `diag_blocks`: each block is a diagonal with entries from 1 to 3 plus small dense noise.
All inputs are finite; a program needn't handle non-finite values.
Results may differ from a plain program's by a relative error of at most 0.028.
Values may be sent and summed in bfloat16 or wider, within the bound.
No kernel may reach another device: no remote copies, remote signals or barrier semaphores. Data moves between devices by JAX's collectives and lax.ppermute only.
A program may use at most 64 MiB of HBM per device.

v0:
```python
import jax
import jax.numpy as jnp
from jax import lax
from jax.sharding import PartitionSpec as P

damping = 0.7


def far_field(
    vector,
    bases,
    leaf_to_middle_transfer,
    mid_transfer,
    leaf_coupling,
    cluster_coupling,
    group_coupling,
    slots,
    cluster_lists,
    group_lists,
):
    single_precision = jnp.float32
    brain_float_sixteen = jnp.bfloat16
    rank = bases.shape[2]
    columns = vector.shape[1]
    leaf_coefficient = jnp.einsum(
        "na,nr->ar", bases[0], vector, preferred_element_type=single_precision
    ).astype(brain_float_sixteen)
    upward_contribution = jnp.einsum(
        "ba,br->ar",
        leaf_to_middle_transfer[0],
        leaf_coefficient,
        preferred_element_type=single_precision,
    ).astype(brain_float_sixteen)
    sibling_coefs = lax.all_gather(leaf_coefficient, "leaf", axis=0, tiled=True).reshape(
        -1, rank, columns
    )
    cluster_coef = lax.psum(
        upward_contribution.astype(single_precision).astype(jnp.bfloat16), "leaf"
    ).astype(jnp.float32)
    cluster_half = cluster_coef.astype(brain_float_sixteen)
    cluster_index = lax.axis_index(("top", "mid"))
    own_transfer = lax.dynamic_index_in_dim(mid_transfer, cluster_index, 0, keepdims=False)
    all_clusters = lax.all_gather(cluster_half, ("top", "mid"), axis=0, tiled=True).reshape(
        -1, rank, columns
    )
    group_terms = jnp.einsum(
        "cba,cbr->car", mid_transfer, all_clusters, preferred_element_type=single_precision
    )
    group_coefs = jnp.sum(
        group_terms.reshape(-1, lax.axis_size("mid"), rank, columns), axis=1
    ).astype(brain_float_sixteen)
    group_far = jnp.einsum(
        "kab,kbr->ar",
        group_coupling[0],
        jnp.take(group_coefs, group_lists[0], axis=0),
        preferred_element_type=single_precision,
    )
    cluster_far = jnp.einsum(
        "kab,kbr->ar",
        cluster_coupling[0],
        jnp.take(all_clusters, cluster_lists[0], axis=0),
        preferred_element_type=single_precision,
    )
    picked = jnp.take(sibling_coefs, slots, axis=0)
    leaf_distant_field = jnp.einsum(
        "kab,kbr->ar", leaf_coupling[0], picked, preferred_element_type=single_precision
    )
    cluster_total = (
        cluster_far
        + jnp.dot(
            own_transfer,
            group_far.astype(brain_float_sixteen),
            preferred_element_type=single_precision,
        )
    ).astype(brain_float_sixteen)
    leaf_grand_total = (
        leaf_distant_field
        + jnp.dot(
            leaf_to_middle_transfer[0], cluster_total, preferred_element_type=single_precision
        )
    ).astype(brain_float_sixteen)
    return jnp.dot(bases[0], leaf_grand_total, preferred_element_type=single_precision)


def body(
    rhs,
    guess,
    diag_blocks,
    precond,
    bases,
    leaf_to_middle_transfer,
    mid_transfer,
    leaf_coupling,
    cluster_coupling,
    group_coupling,
    leaf_lists,
    owner,
    cluster_lists,
    group_lists,
):
    slots = jnp.take(owner[0], leaf_lists[0], axis=0)

    def apply_matrix(vector):
        near_part = jnp.dot(diag_blocks[0], vector, preferred_element_type=jnp.float32)
        return near_part + far_field(
            vector,
            bases,
            leaf_to_middle_transfer,
            mid_transfer,
            leaf_coupling,
            cluster_coupling,
            group_coupling,
            slots,
            cluster_lists,
            group_lists,
        )

    def smooth(residual):
        return jnp.dot(
            precond[0], residual.astype(jnp.bfloat16), preferred_element_type=jnp.float32
        )

    target = rhs.astype(jnp.float32)
    residual = target - apply_matrix(guess)
    first = guess.astype(jnp.float32) + damping * smooth(residual)
    residual = target - apply_matrix(first.astype(jnp.bfloat16))
    second = first + damping * smooth(residual)
    return second.astype(jnp.bfloat16)


def solution(mesh):
    in_specs = (
        P(("top", "mid", "leaf"), None),
        P(("top", "mid", "leaf"), None),
        P(("top", "mid", "leaf"), None, None),
        P(("top", "mid", "leaf"), None, None),
        P(("top", "mid", "leaf"), None, None),
        P(("top", "mid", "leaf"), None, None),
        P(),
        P(("top", "mid", "leaf"), None, None, None),
        P(("top", "mid"), None, None, None),
        P("top", None, None, None),
        P(("top", "mid", "leaf"), None),
        P(("top", "mid"), None),
        P(("top", "mid"), None),
        P("top", None),
    )
    out_specs = P(("top", "mid", "leaf"), None)
    return jax.shard_map(body, mesh=mesh, in_specs=in_specs, out_specs=out_specs, check_vma=False)
```

profile of v0, /device:TPU:1, one launch (start us, length us, event | category | flops | bytes accessed | tf_op | source)
XLA Modules:
  0.0 158.7 jit_solution(18310039830741658121)
XLA Ops:
  6.5 0.0 copy-start
  6.5 0.0 all-reduce.3.cloned.1.call-start
  6.6 0.9 copy-done
  7.5 1.5 convolution_convert_fusion.1
  9.0 1.6 fusion.41
  10.6 0.0 all-reduce.3.cloned.1.call-update
  10.6 0.0 all-reduce.5.cloned.1.call-start
  10.7 1.3 compare_and_fusion.1
  11.9 0.7 compare_select_fusion.1
  12.6 0.7 compare_and_fusion
  13.2 0.7 compare_select_fusion
  13.9 13.3 %all_gather.12 = bf16[512,256]{1,0:T(8,128)(2,1)S(1)} all-gather(bf16[128,256]{1,0:T(8,128)(2,1)S(1)} %convolution_convert_fusion.1), channel_id=1, replica_groups=mesh['top'=4,'mid'=2,'leaf'=4] {'leaf'}, dimensions={0}, use_global_device_ids=true | all-gather | bytes 327680 | tf_op jit(solution)/shard_map/all_gather | solution.py:34
  27.2 1.1 copy.41
  28.4 0.6 gather_fusion
  29.1 0.0 copy-start.12
  29.1 4.9 %fusion.6 = f32[1536,256]{1,0:T(8,128)} fusion(bf16[1536,256]{1,0:T(8,128)(2,1)S(1)} %copy-done.3, bf16[1,1536,1536]{2,1,0:T(8,128)(2,1)} %param.22), kind=kOutput, calls=%fused_computation.13 | convolution fusion | flops 1207959552 | bytes 7077888 | tf_op jit(solution)/shard_map/dot_general | solution.py:104
  34.0 0.6 gather_fusion.1
  34.6 1.0 convolution_bitcast_fusion.2
  35.6 9.6 %all-reduce.3.cloned.1.call-done = bf16[128,256]{0,1:T(8,128)(2,1)} async-done(((bf16[128,256]{0,1:T(8,128)(2,1)}), bf16[128,256]{0,1:T(8,128)(2,1)}) %all-reduce.3.cloned.1.call-update) | async-done | bytes 65552 | tf_op jit(solution)/shard_map/psum | solution.py:37
  45.2 20.7 %all_gather.13 = bf16[1024,256]{0,1:T(8,128)(2,1)S(1)} all-gather(bf16[128,256]{0,1:T(8,128)(2,1)} %all-reduce.3.cloned.1.call-done), channel_id=1, replica_groups=mesh['top'=4,'mid'=2,'leaf'=4] {'top','mid'}, dimensions={0}, use_global_device_ids=true | all-gather | bytes 589824 | tf_op jit(solution)/shard_map/all_gather | solution.py:43
  65.9 0.2 copy.67
  66.1 1.3 gather_fusion.2
  67.3 1.1 bitcast_reduce_fusion.1
  68.4 1.5 gather_fusion.3
  69.9 1.3 convolution_bitcast_fusion.6
  71.2 1.2 fusion.37
  72.5 2.4 %fusion.33 = bf16[1536,256]{1,0:T(8,128)(2,1)} fusion(f32[1536,256]{1,0:T(8,128)S(1)} %copy-done.5, bf16[1536,256]{1,0:T(8,128)(2,1)S(1)} %copy-done.2, f32[256,128]{1,0:T(8,128)} %convolution_bitcast_fusion.2, bf16[128,256]{0,1:T(8,128)(2,1)S(1)} %fusion.37, bf16[1,1536,128]{2,1,0:T(8,128)(2,1)S(1)} %copy-done, bf16[1,128,128]{2,1,0:T(8,128)(2,1)} %param.25), kind=kOutput, calls=%fused_computation.28 | convolution fusion | flops 110690304 | bytes 3768320 | tf_op jit(solution)/shard_map/dot_general | solution.py:82
  74.8 4.2 %fusion.24 = f32[1536,256]{0,1:T(8,128)S(1)} fusion(bf16[1536,256]{1,0:T(8,128)(2,1)} %fusion.33, bf16[1,1536,1536]{2,1,0:T(8,128)(2,1)} %param.23, bf16[1536,256]{0,1:T(8,128)(2,1)} %copy.41), kind=kOutput, calls=%fused_computation.25 | convolution fusion | flops 1209139200 | bytes 7864320 | tf_op jit(solution)/shard_map/dot_general | solution.py:119
  79.1 0.4 convolution_convert_fusion
  79.4 0.0 copy-start.8
  79.4 5.1 %fusion.4 = f32[256,1536]{0,1:T(8,128)} fusion(bf16[1,1536,1536]{2,1,0:T(8,128)(2,1)} %param.22, f32[1536,256]{0,1:T(8,128)S(1)} %fusion.24), kind=kOutput, calls=%fused_computation.11 | convolution fusion | flops 1208352768 | bytes 7864320 | tf_op jit(solution)/shard_map/dot_general | solution.py:104
  84.6 0.8 fusion.42
  85.4 0.0 all-reduce.5.cloned.1.call-update
  85.4 11.6 %all_gather.14 = bf16[512,256]{0,1:T(8,128)(2,1)S(1)} all-gather(bf16[128,256]{0,1:T(8,128)(2,1)S(1)} %bitcast.168), channel_id=1, replica_groups=mesh['top'=4,'mid'=2,'leaf'=4] {'leaf'}, dimensions={0}, use_global_device_ids=true | all-gather | bytes 327680 | tf_op jit(solution)/shard_map/all_gather | solution.py:34
  97.0 0.1 copy.66
  97.1 0.6 gather_fusion.4
  97.7 1.0 convolution_bitcast_fusion.1
  98.7 17.8 %all-reduce.5.cloned.1.call-done = bf16[128,256]{0,1:T(8,128)(2,1)} async-done(((bf16[128,256]{0,1:T(8,128)(2,1)}), bf16[128,256]{0,1:T(8,128)(2,1)}) %all-reduce.5.cloned.1.call-update) | async-done | bytes 65552 | tf_op jit(solution)/shard_map/psum | solution.py:37
  116.5 20.7 %all_gather.15 = bf16[1024,256]{0,1:T(8,128)(2,1)S(1)} all-gather(bf16[128,256]{0,1:T(8,128)(2,1)} %all-reduce.5.cloned.1.call-done), channel_id=1, replica_groups=mesh['top'=4,'mid'=2,'leaf'=4] {'top','mid'}, dimensions={0}, use_global_device_ids=true | all-gather | bytes 589824 | tf_op jit(solution)/shard_map/all_gather | solution.py:43
  137.2 0.2 copy.68
  137.4 1.2 gather_fusion.5
  138.7 1.1 bitcast_reduce_fusion
  139.7 1.5 gather_fusion.6
  141.3 1.3 convolution_bitcast_fusion.4
  142.6 1.2 fusion.39
  143.8 2.4 %fusion.34 = bf16[1536,256]{1,0:T(8,128)(2,1)} fusion(f32[256,1536]{0,1:T(8,128)S(1)} %copy-done.4, bf16[1536,256]{1,0:T(8,128)(2,1)S(1)} %copy-done.2, f32[256,128]{1,0:T(8,128)} %convolution_bitcast_fusion.1, bf16[128,256]{0,1:T(8,128)(2,1)S(1)} %fusion.39, bf16[1,1536,128]{2,1,0:T(8,128)(2,1)S(1)} %copy-done, bf16[1,128,128]{2,1,0:T(8,128)(2,1)} %param.25), kind=kOutput, calls=%fused_computation.29 | convolution fusion | flops 110690304 | bytes 3768320 | tf_op jit(solution)/shard_map/dot_general | solution.py:82
  146.2 4.5 %fusion.30 = bf16[1536,256]{0,1:T(8,128)(2,1)S(1)} fusion(f32[1536,256]{0,1:T(8,128)} %copy-done.6, bf16[1536,256]{1,0:T(8,128)(2,1)} %fusion.34, bf16[1,1536,1536]{2,1,0:T(8,128)(2,1)} %param.23), kind=kOutput, calls=%fused_computation.27 | convolution fusion | flops 1209139200 | bytes 7864320 | tf_op jit(solution)/shard_map/dot_general | solution.py:119
  150.7 1.2 copy.56
  (32 shorter events, 0.1 us)
Async XLA Ops:
  6.5 1.0 copy-start
  6.5 20.7 %copy-start.3 = (bf16[1536,256]{1,0:T(8,128)(2,1)S(1)}, bf16[1536,256]{1,0:T(8,128)(2,1)}, u32[]{:S(2)}) copy-start(bf16[1536,256]{1,0:T(8,128)(2,1)} %param.21) | copy-start | bytes 2359300
  6.5 21.8 %copy-start.9 = (s32[1,4]{1,0:T(1,128)S(1)}, s32[1,4]{1,0:T(1,128)}, u32[]{:S(2)}) copy-start(s32[1,4]{1,0:T(1,128)} %param.30) | copy-start | bytes 52
  6.5 21.9 %copy-start.1 = (s32[1,4]{1,0:T(1,128)S(1)}, s32[1,4]{1,0:T(1,128)}, u32[]{:S(2)}) copy-start(s32[1,4]{1,0:T(1,128)} %param.31) | copy-start | bytes 52
  6.5 38.6 %all-reduce.3.cloned.1.call-start = ((), (), s32[]{:S(2)}) async-start(), calls=%async_computation | async-start | bytes 131072 | tf_op jit(solution)/shard_map/psum | solution.py:37
  10.6 105.9 %all-reduce.5.cloned.1.call-start = ((), (), s32[]{:S(2)}) async-start(), calls=%async_computation.1 | async-start | bytes 131072 | tf_op jit(solution)/shard_map/psum | solution.py:37
  29.1 5.5 %copy-start.10 = (pred[4]{0:T(512)(128)(4,1)}, pred[4]{0:T(512)(128)(4,1)S(1)}, u32[]{:S(2)}) copy-start(pred[4]{0:T(512)(128)(4,1)S(1)} %get-tuple-element.6) | copy-start | bytes 16
  29.1 5.5 %copy-start.12 = (bf16[1,4,128,128]{3,2,1,0:T(8,128)(2,1)S(1)}, bf16[1,4,128,128]{3,2,1,0:T(8,128)(2,1)}, u32[]{:S(2)}) copy-start(bf16[1,4,128,128]{3,2,1,0:T(8,128)(2,1)} %param.27) | copy-start | bytes 393220
  34.0 33.3 %copy-start.7 = (bf16[8,128,128]{2,1,0:T(8,128)(2,1)S(1)}, bf16[8,128,128]{2,1,0:T(8,128)(2,1)}, u32[]{:S(2)}) copy-start(bf16[8,128,128]{2,1,0:T(8,128)(2,1)} %param.26) | copy-start | bytes 786436
  65.9 6.6 %copy-start.2 = (bf16[1536,256]{1,0:T(8,128)(2,1)S(1)}, bf16[1536,256]{1,0:T(8,128)(2,1)}, u32[]{:S(2)}) copy-start(bf16[1536,256]{1,0:T(8,128)(2,1)} %param.20) | copy-start | bytes 2359300
  66.1 6.4 %copy-start.5 = (f32[1536,256]{1,0:T(8,128)S(1)}, f32[1536,256]{1,0:T(8,128)}, u32[]{:S(2)}) copy-start(f32[1536,256]{1,0:T(8,128)} %fusion.6) | copy-start | bytes 4718596
  79.1 5.5 %copy-start.6 = (f32[1536,256]{0,1:T(8,128)}, f32[1536,256]{0,1:T(8,128)S(1)}, u32[]{:S(2)}) copy-start(f32[1536,256]{0,1:T(8,128)S(1)} %fusion.24) | copy-start | bytes 4718596
  79.4 5.1 %copy-start.8 = (bf16[1,128,128]{2,1,0:T(8,128)(2,1)S(1)}, bf16[1,128,128]{2,1,0:T(8,128)(2,1)}, u32[]{:S(2)}) copy-start(bf16[1,128,128]{2,1,0:T(8,128)(2,1)} %param.25) | copy-start | bytes 98308
  84.6 13.1 %copy-start.11 = (pred[4]{0:T(512)(128)(4,1)S(1)}, pred[4]{0:T(512)(128)(4,1)}, u32[]{:S(2)}) copy-start(pred[4]{0:T(512)(128)(4,1)} %copy-done.10) | copy-start | bytes 16
  84.6 13.2 %copy-start.13 = (bf16[1,4,128,128]{3,2,1,0:T(8,128)(2,1)S(1)}, bf16[1,4,128,128]{3,2,1,0:T(8,128)(2,1)}, u32[]{:S(2)}) copy-start(bf16[1,4,128,128]{3,2,1,0:T(8,128)(2,1)} %param.27) | copy-start | bytes 393220
  98.7 42.6 %copy-start.14 = (pred[3]{0:T(512)(128)(4,1)S(1)}, pred[3]{0:T(512)(128)(4,1)}, u32[]{:S(2)}) copy-start(pred[3]{0:T(512)(128)(4,1)} %compare_and_fusion.1) | copy-start | bytes 13
  137.4 6.4 %copy-start.4 = (f32[256,1536]{0,1:T(8,128)S(1)}, f32[256,1536]{0,1:T(8,128)}, u32[]{:S(2)}) copy-start(f32[256,1536]{0,1:T(8,128)} %fusion.4) | copy-start | bytes 4718596
Sparse Core Ops, SparseCore 0:
  10.7 34.4 all-reduce.2
  85.5 31.0 all-reduce.4
where the time goes:
time: 159 us
  blocking collectives  66.3 us (42%)
  matrix products  36.8 us (23%)
  waiting for transfers between devices  27.4 us (17%)
  between operations  13.7 us (9%)
  local copies, waits for them, and re-layouts  11.1 us (7%)
  other arithmetic  3.27 us (2%)
    all_gather x2, blocking collectives, far_field(): lax.all_gather(cluster_half, ('top', 'mid'), axis=0, tiled=True)  41.3 us
    psum x2, waiting for transfers between devices, far_field(): lax.psum(upward_contribution.astype(single_precision).astype(jnp.bfloat16...  27.4 us
    all_gather x2, blocking collectives, far_field(): lax.all_gather(leaf_coefficient, 'leaf', axis=0, tiled=True)  25 us
    dot_general x2, matrix products, apply_matrix(): jnp.dot(diag_blocks[0], vector, preferred_element_type=jnp.float32)  10 us
    dot_general x2, matrix products, smooth(): jnp.dot(precond[0], residual.astype(jnp.bfloat16), preferred_element_type...  8.73 us
    dot_general x2, matrix products, far_field(): jnp.dot(bases[0], leaf_grand_total, preferred_element_type=single_precision)  4.72 us
  transfers between devices with their start and end apart: 2, of which 2 were waited for; matrix products, arithmetic and copies ran while one was open for 8% of the time, Pallas kernels for 0%

commit v1 on v0

--- a/solution.py
+++ b/solution.py
@@ -34,8 +34,9 @@
     sibling_coefs = lax.all_gather(leaf_coefficient, "leaf", axis=0, tiled=True).reshape(
         -1, rank, columns
     )
-    cluster_coef = lax.psum(
-        upward_contribution.astype(single_precision).astype(jnp.bfloat16), "leaf"
+    cluster_coef = jnp.sum(
+        lax.all_gather(upward_contribution.astype(single_precision).astype(jnp.bfloat16), "leaf"),
+        axis=0,
     ).astype(jnp.float32)
     cluster_half = cluster_coef.astype(brain_float_sixteen)
     cluster_index = lax.axis_index(("top", "mid"))

time: 159 us -> 132 us (0.83)
  waiting for transfers between devices: 27.4 us -> 0 us
  blocking collectives: 66.3 us -> 90.3 us
  between operations: 13.7 us -> 0.38 us
  matrix products: 36.8 us -> 26.8 us
  local copies, waits for them, and re-layouts: 11.1 us -> 9.25 us
    psum x2 -> x0, waiting for transfers between devices: 27.4 us -> none  [far_field(): lax.psum(upward_contribution.astype(single_precision).astype(jnp.bfloat16...]
    all_gather x0 -> x2, blocking collectives: none -> 21.1 us  [far_field(): lax.all_gather(upward_contribution.astype(single_precision).astype(jnp.bf...]
    all_gather x2, blocking collectives: 41.3 us -> 44.6 us  [far_field(): lax.all_gather(cluster_half, ('top', 'mid'), axis=0, tiled=True)]
    dot_general x2, matrix products: 2.37 us -> 0.33 us  [far_field(): jnp.einsum('ba,br->ar', leaf_to_middle_transfer[0], leaf_coefficient, pre...]
    dot_general x2, matrix products: 10 us -> 8.03 us  [apply_matrix(): jnp.dot(diag_blocks[0], vector, preferred_element_type=jnp.float32)]
    dot_general x2, matrix products: 2.61 us -> 0.63 us  [far_field(): jnp.einsum('kab,kbr->ar', cluster_coupling[0], jnp.take(all_clusters, clu...]
    gather x2, local copies, waits for them, and re-layouts: 3.04 us -> 1.15 us  [far_field(): jnp.take(group_coefs, group_lists[0], axis=0)]
    dot_general x2, matrix products: 4.72 us -> 3.03 us  [far_field(): jnp.dot(bases[0], leaf_grand_total, preferred_element_type=single_precision)]
  transfers between devices with their start and end apart: 2 -> 0, of which waited for: 2 -> 0; matrix products, arithmetic and copies ran while one was open for 8% -> 0% of each run, Pallas kernels for 0% -> 0%
where the time goes in v1:
time: 132 us; the launch traced here: 131 us
  blocking collectives  90.3 us (68%)
  matrix products  26.8 us (20%)
  local copies, waits for them, and re-layouts  9.25 us (7%)
  other arithmetic  4.69 us (4%)
    all_gather x2, blocking collectives, far_field(): lax.all_gather(cluster_half, ('top', 'mid'), axis=0, tiled=True)  44.6 us
    all_gather x2, blocking collectives, far_field(): lax.all_gather(leaf_coefficient, 'leaf', axis=0, tiled=True)  24.5 us
    all_gather x2, blocking collectives, far_field(): lax.all_gather(upward_contribution.astype(single_precision).astype(jnp.bf...  21.1 us
    dot_general x2, matrix products, smooth(): jnp.dot(precond[0], residual.astype(jnp.bfloat16), preferred_element_type...  8.27 us
    dot_general x2, matrix products, apply_matrix(): jnp.dot(diag_blocks[0], vector, preferred_element_type=jnp.float32)  8.03 us
    dot_general x2, matrix products, far_field(): jnp.dot(bases[0], leaf_grand_total, preferred_element_type=single_precision)  3.03 us
    unnamed x37, local copies, waits for them, and re-layouts  2.74 us

profile of v1, /device:TPU:1, one launch (start us, length us, event | category | flops | bytes accessed | tf_op | source)
XLA Modules:
  0.0 131.4 jit_solution(12813554577486661431)
XLA Ops:
  0.0 0.7 compare_and_fusion.1
  0.7 0.7 compare_and_fusion
  1.4 0.7 fusion.91
  2.1 0.7 compare_select_fusion.1
  2.7 0.7 compare_select_fusion
  3.4 1.3 gather_fusion
  4.7 0.7 compare_and_fusion.2
  5.4 1.5 %convolution_convert_fusion.1 = bf16[128,256]{1,0:T(8,128)(2,1)S(1)} fusion(bf16[1536,256]{1,0:T(8,128)(2,1)} %param.21, bf16[1,1536,128]{2,1,0:T(8,128)(2,1)S(1)} %copy-done), kind=kOutput, calls=%fused_computation.41 | convolution fusion | flops 100696064 | bytes 1245184 | tf_op jit(solution)/shard_map/na,nr->ar/dot_general | solution.py:25
  6.9 0.2 fusion.41
  7.1 13.3 %all_gather.24 = bf16[512,256]{1,0:T(8,128)(2,1)S(1)} all-gather(bf16[128,256]{1,0:T(8,128)(2,1)S(1)} %convolution_convert_fusion.1), channel_id=1, replica_groups=mesh['top'=4,'mid'=2,'leaf'=4] {'leaf'}, dimensions={0}, use_global_device_ids=true | all-gather | bytes 327680 | tf_op jit(solution)/shard_map/all_gather | solution.py:34
  20.4 0.6 gather_fusion.1
  20.9 1.0 convolution_bitcast_fusion.2
  21.9 10.3 %all-gather = bf16[512,256]{0,1:T(8,128)(2,1)S(1)} all-gather(bf16[128,256]{0,1:T(8,128)(2,1)S(1)} %fusion.41), channel_id=2, replica_groups=mesh['top'=4,'mid'=2,'leaf'=4] {'leaf'}, dimensions={0}, use_global_device_ids=true | all-gather | bytes 327680 | tf_op jit(solution)/shard_map/all_gather | solution.py:38
  32.3 0.1 reshape.129
  32.3 0.3 reduce_sum.42
  32.7 23.7 %all_gather.27 = bf16[1024,256]{0,1:T(8,128)(2,1)S(1)} all-gather(bf16[128,256]{0,1:T(8,128)(2,1)S(1)} %reduce_sum.42), channel_id=1, replica_groups=mesh['top'=4,'mid'=2,'leaf'=4] {'top','mid'}, dimensions={0}, use_global_device_ids=true | all-gather | bytes 589824 | tf_op jit(solution)/shard_map/all_gather | solution.py:44
  56.4 0.2 copy.39
  56.6 0.6 gather_fusion.2
  57.2 0.3 bitcast_reduce_fusion.1
  57.5 0.6 gather_fusion.3
  58.1 0.3 convolution_bitcast_fusion.6
  58.4 1.0 fusion.37
  59.4 1.2 copy.37
  60.6 3.8 %fusion.6 = f32[1536,256]{1,0:T(8,128)S(1)} fusion(bf16[1536,256]{1,0:T(8,128)(2,1)S(1)} %copy-done.2, bf16[1,1536,1536]{2,1,0:T(8,128)(2,1)} %param.22), kind=kOutput, calls=%fused_computation.13 | convolution fusion | flops 1207959552 | bytes 7077888 | tf_op jit(solution)/shard_map/dot_general | solution.py:105
  64.4 1.5 %fusion.33 = bf16[1536,256]{1,0:T(8,128)(2,1)S(1)} fusion(f32[1536,256]{1,0:T(8,128)S(1)} %fusion.6, bf16[1536,256]{1,0:T(8,128)(2,1)S(1)} %copy-done.1, f32[256,128]{1,0:T(8,128)} %convolution_bitcast_fusion.2, bf16[128,256]{0,1:T(8,128)(2,1)} %fusion.37, bf16[1,1536,128]{2,1,0:T(8,128)(2,1)S(1)} %copy-done, bf16[1,128,128]{2,1,0:T(8,128)(2,1)} %param.25), kind=kOutput, calls=%fused_computation.28 | convolution fusion | flops 110690304 | bytes 3768320 | tf_op jit(solution)/shard_map/dot_general | solution.py:83
  65.9 4.0 %fusion.24 = f32[1536,256]{0,1:T(8,128)S(1)} fusion(bf16[1536,256]{1,0:T(8,128)(2,1)S(1)} %fusion.33, bf16[1,1536,1536]{2,1,0:T(8,128)(2,1)} %param.23, bf16[1536,256]{0,1:T(8,128)(2,1)} %copy.37), kind=kOutput, calls=%fused_computation.25 | convolution fusion | flops 1209139200 | bytes 7864320 | tf_op jit(solution)/shard_map/dot_general | solution.py:120
  69.9 1.1 copy-done.3
  71.1 0.4 convolution_convert_fusion
  71.5 0.4 copy-done.7
  71.8 0.1 fusion.42
  72.0 10.8 %all-gather.1 = bf16[512,256]{0,1:T(8,128)(2,1)S(1)} all-gather(bf16[128,256]{0,1:T(8,128)(2,1)S(1)} %fusion.42), channel_id=3, replica_groups=mesh['top'=4,'mid'=2,'leaf'=4] {'leaf'}, dimensions={0}, use_global_device_ids=true | all-gather | bytes 327680 | tf_op jit(solution)/shard_map/all_gather | solution.py:38
  82.8 0.1 reshape.130
  82.9 0.3 reduce_sum.44
  83.2 11.2 %all_gather.28 = bf16[512,256]{0,1:T(8,128)(2,1)S(1)} all-gather(bf16[128,256]{0,1:T(8,128)(2,1)S(1)} %bitcast.172), channel_id=1, replica_groups=mesh['top'=4,'mid'=2,'leaf'=4] {'leaf'}, dimensions={0}, use_global_device_ids=true | all-gather | bytes 327680 | tf_op jit(solution)/shard_map/all_gather | solution.py:34
  94.5 0.1 copy.64
  94.6 0.6 gather_fusion.4
  95.2 1.0 convolution_bitcast_fusion.1
  96.2 20.9 %all_gather.31 = bf16[1024,256]{0,1:T(8,128)(2,1)S(1)} all-gather(bf16[128,256]{0,1:T(8,128)(2,1)S(1)} %reduce_sum.44), channel_id=1, replica_groups=mesh['top'=4,'mid'=2,'leaf'=4] {'top','mid'}, dimensions={0}, use_global_device_ids=true | all-gather | bytes 589824 | tf_op jit(solution)/shard_map/all_gather | solution.py:44
  117.1 0.2 copy.46
  117.3 0.6 gather_fusion.5
  117.9 0.3 bitcast_reduce_fusion
  118.3 0.6 gather_fusion.6
  118.9 0.3 convolution_bitcast_fusion.4
  119.2 1.0 fusion.39
  120.2 4.2 %fusion.4 = f32[256,1536]{0,1:T(8,128)S(1)} fusion(bf16[1,1536,1536]{2,1,0:T(8,128)(2,1)} %param.22, f32[1536,256]{0,1:T(8,128)} %copy-done.3), kind=kOutput, calls=%fused_computation.11 | convolution fusion | flops 1208352768 | bytes 7864320 | tf_op jit(solution)/shard_map/dot_general | solution.py:105
  124.4 1.5 %fusion.34 = bf16[1536,256]{1,0:T(8,128)(2,1)S(1)} fusion(f32[256,1536]{0,1:T(8,128)S(1)} %fusion.4, bf16[1536,256]{1,0:T(8,128)(2,1)S(1)} %copy-done.1, f32[256,128]{1,0:T(8,128)} %convolution_bitcast_fusion.1, bf16[128,256]{0,1:T(8,128)(2,1)} %fusion.39, bf16[1,1536,128]{2,1,0:T(8,128)(2,1)S(1)} %copy-done, bf16[1,128,128]{2,1,0:T(8,128)(2,1)} %param.25), kind=kOutput, calls=%fused_computation.29 | convolution fusion | flops 110690304 | bytes 3768320 | tf_op jit(solution)/shard_map/dot_general | solution.py:83
  126.0 4.3 %fusion.30 = bf16[1536,256]{0,1:T(8,128)(2,1)S(1)} fusion(f32[1536,256]{0,1:T(8,128)} %copy-done.3, bf16[1536,256]{1,0:T(8,128)(2,1)S(1)} %fusion.34, bf16[1,1536,1536]{2,1,0:T(8,128)(2,1)} %param.23), kind=kOutput, calls=%fused_computation.27 | convolution fusion | flops 1209139200 | bytes 7864320 | tf_op jit(solution)/shard_map/dot_general | solution.py:120
  130.2 1.2 copy.52
  (38 shorter events, 0.1 us)
Async XLA Ops:
  0.0 5.4 %copy-start = (bf16[1,1536,128]{2,1,0:T(8,128)(2,1)S(1)}, bf16[1,1536,128]{2,1,0:T(8,128)(2,1)}, u32[]{:S(2)}) copy-start(bf16[1,1536,128]{2,1,0:T(8,128)(2,1)} %param.24) | copy-start | bytes 1179652
  0.0 6.9 %copy-start.6 = (bf16[1,128,128]{2,1,0:T(8,128)(2,1)S(1)}, bf16[1,128,128]{2,1,0:T(8,128)(2,1)}, u32[]{:S(2)}) copy-start(bf16[1,128,128]{2,1,0:T(8,128)(2,1)} %param.25) | copy-start | bytes 98308
  0.0 20.9 %copy-start.12 = (bf16[1,4,128,128]{3,2,1,0:T(8,128)(2,1)S(1)}, bf16[1,4,128,128]{3,2,1,0:T(8,128)(2,1)}, u32[]{:S(2)}) copy-start(bf16[1,4,128,128]{3,2,1,0:T(8,128)(2,1)} %param.27) | copy-start | bytes 393220
  0.7 57.4 %copy-start.16 = (pred[3]{0:T(512)(128)(4,1)}, pred[3]{0:T(512)(128)(4,1)S(1)}, u32[]{:S(2)}) copy-start(pred[3]{0:T(512)(128)(4,1)S(1)} %compare_and_fusion.1) | copy-start | bytes 13
  5.4 16.6 %copy-start.10 = (pred[4]{0:T(512)(128)(4,1)}, pred[4]{0:T(512)(128)(4,1)S(1)}, u32[]{:S(2)}) copy-start(pred[4]{0:T(512)(128)(4,1)S(1)} %get-tuple-element.6) | copy-start | bytes 16
  21.9 35.2 %copy-start.4 = (bf16[8,128,128]{2,1,0:T(8,128)(2,1)S(1)}, bf16[8,128,128]{2,1,0:T(8,128)(2,1)}, u32[]{:S(2)}) copy-start(bf16[8,128,128]{2,1,0:T(8,128)(2,1)} %param.26) | copy-start | bytes 786436
  32.7 25.4 %copy-start.14 = (bf16[1,3,128,128]{3,2,1,0:T(8,128)(2,1)S(1)}, bf16[1,3,128,128]{3,2,1,0:T(8,128)(2,1)}, u32[]{:S(2)}) copy-start(bf16[1,3,128,128]{3,2,1,0:T(8,128)(2,1)} %param.28) | copy-start | bytes 294916
  56.4 2.1 %copy-start.8 = (bf16[1,2,128,128]{3,2,1,0:T(8,128)(2,1)S(1)}, bf16[1,2,128,128]{3,2,1,0:T(8,128)(2,1)}, u32[]{:S(2)}) copy-start(bf16[1,2,128,128]{3,2,1,0:T(8,128)(2,1)} %param.29) | copy-start | bytes 196612
  56.4 3.1 %copy-start.2 = (bf16[1536,256]{1,0:T(8,128)(2,1)S(1)}, bf16[1536,256]{1,0:T(8,128)(2,1)}, u32[]{:S(2)}) copy-start(bf16[1536,256]{1,0:T(8,128)(2,1)} %param.21) | copy-start | bytes 2359300
  60.6 3.8 %copy-start.1 = (bf16[1536,256]{1,0:T(8,128)(2,1)S(1)}, bf16[1536,256]{1,0:T(8,128)(2,1)}, u32[]{:S(2)}) copy-start(bf16[1536,256]{1,0:T(8,128)(2,1)} %param.20) | copy-start | bytes 2359300
  69.9 1.1 copy-start.3
  71.1 0.8 copy-start.7
  71.4 23.7 %copy-start.11 = (pred[4]{0:T(512)(128)(4,1)S(1)}, pred[4]{0:T(512)(128)(4,1)}, u32[]{:S(2)}) copy-start(pred[4]{0:T(512)(128)(4,1)} %copy-done.10) | copy-start | bytes 16
  71.5 23.7 %copy-start.13 = (bf16[1,4,128,128]{3,2,1,0:T(8,128)(2,1)S(1)}, bf16[1,4,128,128]{3,2,1,0:T(8,128)(2,1)}, u32[]{:S(2)}) copy-start(bf16[1,4,128,128]{3,2,1,0:T(8,128)(2,1)} %param.27) | copy-start | bytes 393220
  94.6 23.3 %copy-start.5 = (bf16[8,128,128]{2,1,0:T(8,128)(2,1)S(1)}, bf16[8,128,128]{2,1,0:T(8,128)(2,1)}, u32[]{:S(2)}) copy-start(bf16[8,128,128]{2,1,0:T(8,128)(2,1)} %param.26) | copy-start | bytes 786436
  96.2 22.7 %copy-start.15 = (bf16[1,3,128,128]{3,2,1,0:T(8,128)(2,1)S(1)}, bf16[1,3,128,128]{3,2,1,0:T(8,128)(2,1)}, u32[]{:S(2)}) copy-start(bf16[1,3,128,128]{3,2,1,0:T(8,128)(2,1)} %param.28) | copy-start | bytes 294916
  96.2 22.7 %copy-start.17 = (pred[3]{0:T(512)(128)(4,1)S(1)}, pred[3]{0:T(512)(128)(4,1)}, u32[]{:S(2)}) copy-start(pred[3]{0:T(512)(128)(4,1)} %copy-done.16) | copy-start | bytes 13
  117.1 2.1 %copy-start.9 = (bf16[1,2,128,128]{3,2,1,0:T(8,128)(2,1)S(1)}, bf16[1,2,128,128]{3,2,1,0:T(8,128)(2,1)}, u32[]{:S(2)}) copy-start(bf16[1,2,128,128]{3,2,1,0:T(8,128)(2,1)} %param.29) | copy-start | bytes 196612
